TPU v7x, 32 devices: a whole 2x2x4 slice. The times are simulated.
32 devices in a mesh: blk: 8 (over z, y), col: 4 (over x, core).
Axes of the slice: x: 2, y: 2, z: 4, core: 2. Of those that a mesh axis runs over, the one named last changes fastest.
Arguments:
- direct_init: float32 [5, 8, 4096], P(None, 'col', 'blk'), may hold values from -6 to 6
- adjoint_init: float32 [5, 8, 4096], P(None, 'col', 'blk'), may hold values from -6 to 6
- jacobian: float32 [5, 5], replicated, may hold values from -2.5 to 2.5
- areas: float32 [6, 4096], P(None, 'blk'), may hold values from 0.5 to 2
- volumes: float32 [4096], P('blk'), may hold values from 2 to 8
- neighbours: int32 [6, 4096], P(None, 'blk'), may hold values from -128 to 128, as said below
- block_cells: int32 [32], P('blk'), may hold values from 32 to 128, as said below
- bank: bfloat16 [128, 5, 4096], P('col', None, 'blk'), may hold values from -6 to 6
Outputs:
- hankel_pair: float32 [8, 8], P(None, 'col')
- hankel_bank: float32 [8, 128], P(None, 'col')
Inputs may be any that keep to these rules, and one draw needn't show every extreme that they name: `neighbours`: each entry is 0 or an offset whose target cell lies inside the mesh; some entries are exactly 128 and -128. `block_cells`: every seventh block is full.
All inputs are finite; a program needn't handle non-finite values.
Results may differ from a plain program's by a relative error of at most 0.0003.
The roundings to bfloat16 on the way count: a program that leaves them out, or rounds other values in their place, can miss the bound.
Values may be sent and summed in bfloat16 or wider, within the bound.
A program may use at most 64 MiB of HBM per device.

v0:
```python
import functools

import jax
import jax.numpy as jnp
from jax import lax
from jax.experimental import pallas as pl
from jax.experimental.pallas import tpu as pltpu
from jax.sharding import PartitionSpec as P

STEPS = 3
TIME_STEP = 0.1
LANES = 128
ROWS = 32
SLOTS = 8
MESH = pl.DeviceIdType.MESH


def lane_take(values, index):
    return jnp.take_along_axis(values, index, axis=1, mode="promise_in_bounds")


def kernel(
    n_blk, n_col, scale_norm,
    jac, cells, direct, adjoint, areas, volumes, neighbours, bank,
    out,
    ext, state, middle, rates, coef, index, side, coef_sum, mixing, bank_rows, rhs, adj_rows, messages, parts,
    halo_send, halo_recv, col_send, col_recv, sum_send, sum_recv,
):
    fields = direct.shape[0]
    tiles = direct.shape[2] // LANES
    me = lax.axis_index("blk")
    mine = lax.axis_index("col")

    barrier = pltpu.get_barrier_semaphore()

    def greet(axis, own, count):
        def one(step, carry):
            peer = lax.rem(own + step, count)
            pl.semaphore_signal(barrier, inc=1, device_id={axis: peer}, device_id_type=MESH)
            return carry
        lax.fori_loop(1, count, one, 0, unroll=count <= 16)

    greet("blk", me, n_blk)
    greet("col", mine, n_col)

    lane = lax.broadcasted_iota(jnp.int32, (1, LANES), 1)
    for t in range(tiles):
        part = pl.ds(t * LANES, LANES)
        live = jnp.where(lane < cells[t], 1.0, 0.0)
        for g in range(fields):
            ext[6 + t, 4 * g:4 * g + 2, :] = direct[g, :, part] * live
            ext[6 + t, 4 * g + 2:4 * g + 4, :] = adjoint[g, :, part] * live
        ext[6 + t, 20:26, :] = live * areas[:, part] / volumes[:, part]
        ext[6 + t, 26:32, :] = neighbours[:, part].astype(jnp.float32)

    pl.semaphore_wait(barrier, n_blk - 1 + n_col - 1)

    hops = (
        (1, (6, 4), (2, 4)),
        (-1, (6, 4), (10, 4)),
        (2, (8, 2), (0, 2)),
        (-2, (6, 2), (14, 2)),
    )

    def halo(k, peer):
        distance, source, target = hops[k]
        return pltpu.make_async_remote_copy(
            src_ref=ext.at[pl.ds(*source)],
            dst_ref=ext.at[pl.ds(*target)],
            send_sem=halo_send.at[k],
            recv_sem=halo_recv.at[k],
            device_id={"blk": peer},
            device_id_type=MESH,
        )

    for k, (distance, source, target) in enumerate(hops):
        goes = (me + distance < n_blk) if distance > 0 else (me + distance >= 0)

        @pl.when(goes)
        def _():
            halo(k, me + distance).start()

        comes = (me - distance >= 0) if distance > 0 else (me - distance < n_blk)

        @pl.when(jnp.logical_not(comes))
        def _():
            ext[pl.ds(*target)] = jnp.zeros((target[1], ROWS, LANES), jnp.float32)

    sub = lax.broadcasted_iota(jnp.int32, (8, LANES), 0)
    is_direct = lax.rem(sub, 4) < 2
    for g in range(fields):
        for h in range(fields):
            mixing[g * fields + h] = jnp.where(is_direct, -jac[g, h], jac[h, g])
    bank_rows[:, 0:fields, :] = bank[...].astype(jnp.float32)
    span = tiles * LANES
    count = bank.shape[0]
    for g in range(fields):
        rhs[0:count, g * span:(g + 1) * span] = bank_rows[:, g, :].astype(jnp.bfloat16)
    adj_rows[...] = jnp.zeros(adj_rows.shape, jnp.float32)

    for k, (distance, source, target) in enumerate(hops):
        comes = (me - distance >= 0) if distance > 0 else (me - distance < n_blk)

        @pl.when(comes)
        def _():
            halo(k, me).wait_recv()

    low = sub < 4

    def both(p, row):
        a = jnp.broadcast_to(ext[p, row:row + 1, :], (8, LANES))
        b = jnp.broadcast_to(ext[15 - p, row:row + 1, :], (8, LANES))
        return jnp.where(low, a, b)

    wide = lax.broadcasted_iota(jnp.int32, (8, LANES), 1)
    for p in range(SLOTS):
        for g in range(fields):
            state[p, g] = jnp.concatenate(
                [ext[p, 4 * g:4 * g + 4, :], ext[15 - p, 4 * g:4 * g + 4, :]], axis=0
            )
        if p == 0:
            continue
        total = jnp.zeros((8, LANES), jnp.float32)
        for f in range(6):
            offset = both(p, 26 + f).astype(jnp.int32)
            c = both(p, 20 + f)
            total = total + c
            coef[p, f] = jnp.where(offset == 0, 0.0, c)
            target = wide + offset
            index[p, f] = jnp.bitwise_and(target, LANES - 1)
            way = jnp.where(target < 0, -1, jnp.where(target >= LANES, 1, 0))
            side[p, f] = jnp.where(low, way, -way)
        coef_sum[p] = total

    def swap_middle(buffer):
        for g in range(fields):
            buffer[SLOTS, g] = pltpu.roll(buffer[SLOTS - 1, g], 4, 0)

    def rate(buffer, p):
        even = [jnp.zeros((8, LANES), jnp.float32) for _ in range(fields)]
        odd = [jnp.zeros((8, LANES), jnp.float32) for _ in range(fields)]
        center = [buffer[p, g] for g in range(fields)]
        for f in range(6):
            ix = index[p, f]
            sd = side[p, f]
            c = coef[p, f]
            outer = sd < 0
            inner = sd > 0
            for g in range(fields):
                got = lane_take(center[g], ix)
                got = jnp.where(outer, lane_take(buffer[p - 1, g], ix), got)
                got = jnp.where(inner, lane_take(buffer[p + 1, g], ix), got)
                if f % 2 == 0:
                    even[g] = even[g] + c * got
                else:
                    odd[g] = odd[g] + c * got
        drift = [even[g] - odd[g] for g in range(fields)]
        result = []
        for g in range(fields):
            value = even[g] + odd[g] - coef_sum[p] * center[g]
            for h in range(fields):
                value = value + mixing[g * fields + h] * drift[h]
            result.append(value)
        return center, result

    for step in range(STEPS):
        swap_middle(state)

        def first(p, carry):
            center, value = rate(state, p)
            for g in range(fields):
                rates[p, g] = value[g]
                middle[p, g] = center[g] + TIME_STEP * value[g]
            return carry

        lax.fori_loop(2 * step + 1, SLOTS, first, 0, unroll=UNROLL)
        swap_middle(middle)

        def second(p, carry):
            _, value = rate(middle, p)
            for g in range(fields):
                state[p, g] = state[p, g] + (0.5 * TIME_STEP) * (rates[p, g] + value[g])
            return carry

        lax.fori_loop(2 * step + 2, SLOTS, second, 0, unroll=UNROLL)

    direct_rows = []
    for g in range(fields):
        for t in range(tiles):
            e = 6 + t
            p, row = (e, 0) if e < SLOTS else (15 - e, 4)
            live = jnp.where(lane < cells[t], 1.0, 0.0)
            weight = volumes[:, t * LANES:(t + 1) * LANES] * live * scale_norm
            column = pl.ds(g * span + t * LANES, LANES)
            direct_rows.append(weight * state[p, g, row:row + 2, :])
            adj_rows[0:2, column] = state[p, g, row + 2:row + 4, :]
    messages[mine] = jnp.concatenate(direct_rows, axis=1).astype(jnp.bfloat16)

    def column_copy(step, slot, peer):
        return pltpu.make_async_remote_copy(
            src_ref=messages.at[slot],
            dst_ref=messages.at[slot],
            send_sem=col_send.at[step],
            recv_sem=col_recv.at[slot],
            device_id={"col": peer},
            device_id_type=MESH,
        )

    for step in range(1, n_col):
        column_copy(step, mine, lax.rem(mine + step, n_col)).start()
    rhs[count:count + 16, :] = adj_rows[...].astype(jnp.bfloat16)
    for step in range(1, n_col):
        slot = lax.rem(mine + step, n_col)
        column_copy(step, slot, slot).wait_recv()

    lhs = jnp.concatenate(
        [messages[c].astype(jnp.float32) for c in range(n_col)], axis=0
    ).astype(jnp.bfloat16)
    product = lax.dot_general(
        lhs, rhs[...], (((1,), (1,)), ((), ())), preferred_element_type=jnp.float32
    )
    parts[me] = product

    def sum_copy(step, slot, peer):
        return pltpu.make_async_remote_copy(
            src_ref=parts.at[slot],
            dst_ref=parts.at[slot],
            send_sem=sum_send.at[step],
            recv_sem=sum_recv.at[slot],
            device_id={"blk": peer},
            device_id_type=MESH,
        )

    def start_sum(step, carry):
        sum_copy(step, me, lax.rem(me + step, n_blk)).start()
        return carry

    def wait_sum(step, carry):
        slot = lax.rem(me + step, n_blk)
        sum_copy(step, slot, slot).wait_recv()
        return carry

    def wait_sent(step, carry):
        sum_copy(step, me, lax.rem(me + step, n_blk)).wait_send()
        return carry

    few = n_blk <= 16
    lax.fori_loop(1, n_blk, start_sum, 0, unroll=few)
    lax.fori_loop(1, n_blk, wait_sum, 0, unroll=few)
    out[...] = lax.fori_loop(
        0, n_blk, lambda i, total: total + parts[i], jnp.zeros(out.shape, jnp.float32), unroll=few
    )

    for k, (distance, source, target) in enumerate(hops):
        goes = (me + distance < n_blk) if distance > 0 else (me + distance >= 0)

        @pl.when(goes)
        def _():
            halo(k, me).wait_send()

    for step in range(1, n_col):
        column_copy(step, mine, mine).wait_send()
    lax.fori_loop(1, n_blk, wait_sent, 0, unroll=few)


UNROLL = True


def local(n_blk, n_col, direct_init, adjoint_init, jacobian, areas, volumes, neighbours, block_cells, bank):
    fields, own, cell_count = direct_init.shape
    count = bank.shape[0]
    wide = fields * cell_count
    scale_norm = (fields * cell_count * n_blk) ** (-0.5)
    vmem = pl.BlockSpec(memory_space=pltpu.VMEM)
    smem = pl.BlockSpec(memory_space=pltpu.SMEM)
    f32 = jnp.float32
    dma = pltpu.SemaphoreType.DMA
    total = pl.pallas_call(
        functools.partial(kernel, n_blk, n_col, scale_norm),
        out_shape=jax.ShapeDtypeStruct((n_col * own, count + 16), f32),
        in_specs=[smem, smem] + [vmem] * 6,
        out_specs=vmem,
        scratch_shapes=[
            pltpu.VMEM((16, ROWS, LANES), f32),
            pltpu.VMEM((SLOTS + 1, fields, 8, LANES), f32),
            pltpu.VMEM((SLOTS + 1, fields, 8, LANES), f32),
            pltpu.VMEM((SLOTS, fields, 8, LANES), f32),
            pltpu.VMEM((SLOTS, 6, 8, LANES), f32),
            pltpu.VMEM((SLOTS, 6, 8, LANES), jnp.int32),
            pltpu.VMEM((SLOTS, 6, 8, LANES), jnp.int32),
            pltpu.VMEM((SLOTS, 8, LANES), f32),
            pltpu.VMEM((fields * fields, 8, LANES), f32),
            pltpu.VMEM((count, 8, cell_count), f32),
            pltpu.VMEM((count + 16, wide), jnp.bfloat16),
            pltpu.VMEM((16, wide), f32),
            pltpu.VMEM((n_col, own, wide), jnp.bfloat16),
            pltpu.VMEM((n_blk, n_col * own, count + 16), f32),
            dma((4,)), dma((4,)), dma((n_col,)), dma((n_col,)), dma((n_blk,)), dma((n_blk,)),
        ],
        compiler_params=pltpu.CompilerParams(collective_id=0, has_side_effects=True),
        name="hankel",
    )(jacobian, block_cells, direct_init, adjoint_init, areas, volumes.reshape(1, cell_count), neighbours, bank)
    return total[:, count:count + own], total[:, :count]


def solution(mesh):
    return jax.shard_map(
        functools.partial(local, mesh.shape["blk"], mesh.shape["col"]),
        mesh=mesh,
        in_specs=(
            P(None, "col", "blk"),
            P(None, "col", "blk"),
            P(),
            P(None, "blk"),
            P("blk"),
            P(None, "blk"),
            P("blk"),
            P("col", None, "blk"),
        ),
        out_specs=(P(None, "col"), P(None, "col")),
        check_vma=False,
    )
```

profile of v0, /device:TPU:0, one launch (start us, length us, event | category | flops | bytes accessed | tf_op | source)
XLA Modules:
  0.0 25.9 jit_solution(4671192570669650935)
XLA Ops:
  0.6 1.7 %copy.10.bank = bf16[32,5,512]{2,1,0:T(8,128)(2,1)} copy(bf16[32,5,512]{2,0,1:T(8,128)(2,1)} %param.15) | data formatting | bytes 327680 | tf_op args[7]
  2.3 21.6 %hankel.1 = f32[8,48]{1,0:T(8,128)} custom-call(f32[5,5]{1,0:T(8,128)} %jac.1, s32[4]{0:T(128)} %cells.1, f32[5,2,512]{2,1,0:T(2,128)} %direct.1, f32[5,2,512]{2,1,0:T(2,128)} %adjoint.1, f32[6,512]{1,0:T(8,128)} %areas.1, f32[1,512]{1,0:T(1,128)} %bitcast.3, s32[6,512]{1,0:T(8,128)} %neighbours.1, bf16[32,5,512]{2,1,0:T(8,128)(2,1)} %copy.10.bank), custom_call_target="tpu_custom_call" | custom-call | tf_op jit(solution)/shard_map/hankel/pallas_call | solution.py:278
  23.9 0.8 %slice.6 = f32[8,2]{1,0:T(8,128)S(1)} slice(f32[8,48]{1,0:T(8,128)} %hankel.1), slice={[0:8], [32:34]} | slice | bytes 128 | tf_op jit(solution)/shard_map/slice | solution.py:303
  24.7 0.0 copy-start
  24.7 0.6 %copy.11 = f32[8,2]{0,1:T(2,128)} copy(f32[8,2]{1,0:T(8,128)S(1)} %slice.6) | data formatting | bytes 128
  25.3 0.0 copy-done
  25.3 0.6 %copy.13 = f32[8,32]{1,0:T(8,128)} copy(f32[8,32]{1,0:T(8,128)S(1)} %bitcast.2) | data formatting | bytes 2048
Async XLA Ops:
  24.7 0.7 %copy-start = (f32[8,48]{1,0:T(8,128)S(1)}, f32[8,48]{1,0:T(8,128)}, u32[]{:S(2)}) copy-start(f32[8,48]{1,0:T(8,128)} %hankel.1) | copy-start | bytes 4612
where the time goes:
time: 26.2 us; the launch traced here: 25.9 us
  Pallas kernels  21.6 us (82%)
  local copies, waits for them, and re-layouts  3.74 us (14%)
  between operations  0.64 us (2%)
    pallas_call x1, Pallas kernels, local(): pl.pallas_call(functools.partial(kernel, n_blk, n_col, scale_norm), out_s...  21.6 us
    unnamed x5, local copies, waits for them, and re-layouts  2.98 us
    slice x1, local copies, waits for them, and re-layouts, local(): return (total[:, count:count + own], total[:, :count])  0.76 us

commit v1 on v0

--- a/solution.py
+++ b/solution.py
@@ -21,9 +21,10 @@
 
 def kernel(
     n_blk, n_col, scale_norm,
-    jac, cells, direct, adjoint, areas, volumes, neighbours, bank,
-    out,
-    ext, state, middle, rates, coef, index, side, coef_sum, mixing, bank_rows, rhs, adj_rows, messages, parts,
+    jac_in, cells_in, direct_in, adjoint_in, areas_in, volumes_in, neighbours_in, bank_in,
+    out_pair, out_bank,
+    ext, state, middle, rates, coef, index, side, coef_sum, mixing, adj_rows, messages, parts,
+    jac, cells, direct, adjoint, areas, volumes, neighbours, bank, loaded,
     halo_send, halo_recv, col_send, col_recv, sum_send, sum_recv,
 ):
     fields = direct.shape[0]
@@ -31,6 +32,16 @@
     me = lax.axis_index("blk")
     mine = lax.axis_index("col")
 
+    loads = [
+        pltpu.make_async_copy(source, target, loaded.at[k])
+        for k, (source, target) in enumerate((
+            (cells_in, cells), (direct_in, direct), (adjoint_in, adjoint), (areas_in, areas),
+            (volumes_in, volumes), (neighbours_in, neighbours), (jac_in, jac), (bank_in, bank),
+        ))
+    ]
+    for load in loads[:6]:
+        load.start()
+
     barrier = pltpu.get_barrier_semaphore()
 
     def greet(axis, own, count):
@@ -42,6 +53,10 @@
 
     greet("blk", me, n_blk)
     greet("col", mine, n_col)
+    for load in loads[6:]:
+        load.start()
+    for load in loads[:6]:
+        load.wait()
 
     lane = lax.broadcasted_iota(jnp.int32, (1, LANES), 1)
     for t in range(tiles):
@@ -86,16 +101,15 @@
         def _():
             ext[pl.ds(*target)] = jnp.zeros((target[1], ROWS, LANES), jnp.float32)
 
+    for load in loads[6:]:
+        load.wait()
     sub = lax.broadcasted_iota(jnp.int32, (8, LANES), 0)
     is_direct = lax.rem(sub, 4) < 2
     for g in range(fields):
         for h in range(fields):
             mixing[g * fields + h] = jnp.where(is_direct, -jac[g, h], jac[h, g])
-    bank_rows[:, 0:fields, :] = bank[...].astype(jnp.float32)
     span = tiles * LANES
-    count = bank.shape[0]
-    for g in range(fields):
-        rhs[0:count, g * span:(g + 1) * span] = bank_rows[:, g, :].astype(jnp.bfloat16)
+    count = bank.shape[1]
     adj_rows[...] = jnp.zeros(adj_rows.shape, jnp.float32)
 
     for k, (distance, source, target) in enumerate(hops):
@@ -208,7 +222,7 @@
 
     for step in range(1, n_col):
         column_copy(step, mine, lax.rem(mine + step, n_col)).start()
-    rhs[count:count + 16, :] = adj_rows[...].astype(jnp.bfloat16)
+    own_adjoint = adj_rows[...].astype(jnp.bfloat16)
     for step in range(1, n_col):
         slot = lax.rem(mine + step, n_col)
         column_copy(step, slot, slot).wait_recv()
@@ -216,10 +230,14 @@
     lhs = jnp.concatenate(
         [messages[c].astype(jnp.float32) for c in range(n_col)], axis=0
     ).astype(jnp.bfloat16)
-    product = lax.dot_general(
-        lhs, rhs[...], (((1,), (1,)), ((), ())), preferred_element_type=jnp.float32
-    )
-    parts[me] = product
+    contract = (((1,), (1,)), ((), ()))
+    bank_part = jnp.zeros((lhs.shape[0], count), jnp.float32)
+    for g in range(fields):
+        bank_part = bank_part + lax.dot_general(
+            lhs[:, g * span:(g + 1) * span], bank[g], contract, preferred_element_type=jnp.float32
+        )
+    pair_part = lax.dot_general(own_adjoint, lhs, contract, preferred_element_type=jnp.float32)
+    parts[me] = jnp.concatenate([bank_part, pair_part[0:8]], axis=1)
 
     def sum_copy(step, slot, peer):
         return pltpu.make_async_remote_copy(
@@ -247,9 +265,11 @@
     few = n_blk <= 16
     lax.fori_loop(1, n_blk, start_sum, 0, unroll=few)
     lax.fori_loop(1, n_blk, wait_sum, 0, unroll=few)
-    out[...] = lax.fori_loop(
-        0, n_blk, lambda i, total: total + parts[i], jnp.zeros(out.shape, jnp.float32), unroll=few
+    total = lax.fori_loop(
+        0, n_blk, lambda i, total: total + parts[i], jnp.zeros(parts.shape[1:], jnp.float32), unroll=few
     )
+    out_bank[...] = total[:, 0:count]
+    out_pair[...] = total[0:out_pair.shape[0], count:count + lhs.shape[0]]
 
     for k, (distance, source, target) in enumerate(hops):
         goes = (me + distance < n_blk) if distance > 0 else (me + distance >= 0)
@@ -264,6 +284,11 @@
 
 
 UNROLL = True
+
+
+def finish(pair_in, bank_in, pair_out, bank_out):
+    pair_out[...] = pair_in[...]
+    bank_out[...] = bank_in[...]
 
 
 def local(n_blk, n_col, direct_init, adjoint_init, jacobian, areas, volumes, neighbours, block_cells, bank):
@@ -272,14 +297,16 @@
     wide = fields * cell_count
     scale_norm = (fields * cell_count * n_blk) ** (-0.5)
     vmem = pl.BlockSpec(memory_space=pltpu.VMEM)
-    smem = pl.BlockSpec(memory_space=pltpu.SMEM)
     f32 = jnp.float32
     dma = pltpu.SemaphoreType.DMA
-    total = pl.pallas_call(
+    pair, projected = pl.pallas_call(
         functools.partial(kernel, n_blk, n_col, scale_norm),
-        out_shape=jax.ShapeDtypeStruct((n_col * own, count + 16), f32),
-        in_specs=[smem, smem] + [vmem] * 6,
-        out_specs=vmem,
+        out_shape=(
+            jax.ShapeDtypeStruct((own, n_col * own), f32),
+            jax.ShapeDtypeStruct((n_col * own, count), f32),
+        ),
+        in_specs=[pl.BlockSpec(memory_space=pl.ANY)] * 8,
+        out_specs=(vmem, vmem),
         scratch_shapes=[
             pltpu.VMEM((16, ROWS, LANES), f32),
             pltpu.VMEM((SLOTS + 1, fields, 8, LANES), f32),
@@ -290,17 +317,34 @@
             pltpu.VMEM((SLOTS, 6, 8, LANES), jnp.int32),
             pltpu.VMEM((SLOTS, 8, LANES), f32),
             pltpu.VMEM((fields * fields, 8, LANES), f32),
-            pltpu.VMEM((count, 8, cell_count), f32),
-            pltpu.VMEM((count + 16, wide), jnp.bfloat16),
             pltpu.VMEM((16, wide), f32),
             pltpu.VMEM((n_col, own, wide), jnp.bfloat16),
-            pltpu.VMEM((n_blk, n_col * own, count + 16), f32),
+            pltpu.VMEM((n_blk, n_col * own, count + n_col * own), f32),
+            pltpu.SMEM(jacobian.shape, f32),
+            pltpu.SMEM(block_cells.shape, jnp.int32),
+            pltpu.VMEM(direct_init.shape, f32),
+            pltpu.VMEM(adjoint_init.shape, f32),
+            pltpu.VMEM(areas.shape, f32),
+            pltpu.VMEM((1, cell_count), f32),
+            pltpu.VMEM(neighbours.shape, jnp.int32),
+            pltpu.VMEM((fields, count, cell_count), jnp.bfloat16),
+            dma((8,)),
             dma((4,)), dma((4,)), dma((n_col,)), dma((n_col,)), dma((n_blk,)), dma((n_blk,)),
         ],
         compiler_params=pltpu.CompilerParams(collective_id=0, has_side_effects=True),
         name="hankel",
-    )(jacobian, block_cells, direct_init, adjoint_init, areas, volumes.reshape(1, cell_count), neighbours, bank)
-    return total[:, count:count + own], total[:, :count]
+    )(jacobian, block_cells, direct_init, adjoint_init, areas, volumes.reshape(1, cell_count), neighbours, bank.transpose(1, 0, 2))
+    pair, projected = pl.pallas_call(
+        finish,
+        out_shape=(
+            jax.ShapeDtypeStruct((own, n_col * own), f32),
+            jax.ShapeDtypeStruct((n_col * own, count), f32),
+        ),
+        in_specs=[vmem, vmem],
+        out_specs=(vmem, vmem),
+        name="finish",
+    )(pair, projected)
+    return pair.T, projected
 
 
 def solution(mesh):

time: 26.2 us -> 22.8 us (0.87)
  local copies, waits for them, and re-layouts: 3.74 us -> 0 us
  Pallas kernels: 21.6 us -> 22 us
    unnamed x5 -> x0, local copies, waits for them, and re-layouts: 2.98 us -> none
    pallas_call x0 -> x1, Pallas kernels: none -> 1.28 us  [local(): pl.pallas_call(finish, out_shape=(jax.ShapeDtypeStruct((own, n_col * own)...]
    pallas_call x1, Pallas kernels: 21.6 us -> 20.7 us  [local(): pl.pallas_call(functools.partial(kernel, n_blk, n_col, scale_norm), out_s...]
    slice x1 -> x0, local copies, waits for them, and re-layouts: 0.76 us -> none  [local(): return (total[:, count:count + own], total[:, :count])]
where the time goes in v1:
time: 22.8 us; the launch traced here: 22.6 us
  Pallas kernels  22 us (96%)
  between operations  0.64 us (3%)
    pallas_call x1, Pallas kernels, local(): pl.pallas_call(functools.partial(kernel, n_blk, n_col, scale_norm), out_s...  20.7 us
    pallas_call x1, Pallas kernels, local(): pl.pallas_call(finish, out_shape=(jax.ShapeDtypeStruct((own, n_col * own)...  1.28 us

profile of v1, /device:TPU:0, one launch (start us, length us, event | category | flops | bytes accessed | tf_op | source)
XLA Modules:
  0.0 22.6 jit_solution(552681213053199270)
XLA Ops:
  0.6 20.7 %hankel.1 = (f32[2,8]{1,0:T(2,128)}, f32[8,32]{1,0:T(8,128)}) custom-call(f32[5,5]{1,0:T(8,128)} %jac_in.1, s32[4]{0:T(128)} %cells_in.1, f32[5,2,512]{2,1,0:T(2,128)} %direct_in.1, f32[5,2,512]{2,1,0:T(2,128)} %adjoint_in.1, f32[6,512]{1,0:T(8,128)} %areas_in.1, f32[1,512]{1,0:T(1,128)} %bitcast.4, s32[6,512]{1,0:T(8,128)} %neighbours_in.1, ...), custom_call_target="tpu_custom_call" | custom-call | tf_op jit(solution)/shard_map/hankel/pallas_call | solution.py:302
  21.4 1.3 %finish.1 = (f32[2,8]{1,0:T(2,128)}, f32[8,32]{1,0:T(8,128)}) custom-call(f32[2,8]{1,0:T(2,128)} %get-tuple-element.6.pair_in, f32[8,32]{1,0:T(8,128)} %get-tuple-element.7.bank_in), custom_call_target="tpu_custom_call" | custom-call | tf_op jit(solution)/shard_map/finish/pallas_call | solution.py:337

commit v2 on v1

--- a/solution.py
+++ b/solution.py
@@ -71,8 +71,10 @@
     pl.semaphore_wait(barrier, n_blk - 1 + n_col - 1)
 
     hops = (
-        (1, (6, 4), (2, 4)),
-        (-1, (6, 4), (10, 4)),
+        (1, (8, 2), (4, 2)),
+        (-1, (6, 2), (10, 2)),
+        (1, (6, 2), (2, 2)),
+        (-1, (8, 2), (12, 2)),
         (2, (8, 2), (0, 2)),
         (-2, (6, 2), (14, 2)),
     )
@@ -112,12 +114,14 @@
     count = bank.shape[1]
     adj_rows[...] = jnp.zeros(adj_rows.shape, jnp.float32)
 
-    for k, (distance, source, target) in enumerate(hops):
-        comes = (me - distance >= 0) if distance > 0 else (me - distance < n_blk)
-
-        @pl.when(comes)
-        def _():
-            halo(k, me).wait_recv()
+    def arrive(ids):
+        for k in ids:
+            distance = hops[k][0]
+            comes = (me - distance >= 0) if distance > 0 else (me - distance < n_blk)
+
+            @pl.when(comes)
+            def _():
+                halo(k, me).wait_recv()
 
     low = sub < 4
 
@@ -127,13 +131,14 @@
         return jnp.where(low, a, b)
 
     wide = lax.broadcasted_iota(jnp.int32, (8, LANES), 1)
-    for p in range(SLOTS):
+
+    def unpack(p):
         for g in range(fields):
             state[p, g] = jnp.concatenate(
                 [ext[p, 4 * g:4 * g + 4, :], ext[15 - p, 4 * g:4 * g + 4, :]], axis=0
             )
         if p == 0:
-            continue
+            return
         total = jnp.zeros((8, LANES), jnp.float32)
         for f in range(6):
             offset = both(p, 26 + f).astype(jnp.int32)
@@ -177,36 +182,44 @@
             result.append(value)
         return center, result
 
-    for step in range(STEPS):
-        swap_middle(state)
-
-        def first(p, carry):
+    def advance(stage, p):
+        if stage % 2:
             center, value = rate(state, p)
             for g in range(fields):
                 rates[p, g] = value[g]
                 middle[p, g] = center[g] + TIME_STEP * value[g]
-            return carry
-
-        lax.fori_loop(2 * step + 1, SLOTS, first, 0, unroll=UNROLL)
-        swap_middle(middle)
-
-        def second(p, carry):
+        else:
             _, value = rate(middle, p)
             for g in range(fields):
                 state[p, g] = state[p, g] + (0.5 * TIME_STEP) * (rates[p, g] + value[g])
-            return carry
-
-        lax.fori_loop(2 * step + 2, SLOTS, second, 0, unroll=UNROLL)
+        if p == SLOTS - 1 and stage < 2 * STEPS:
+            swap_middle(middle if stage % 2 else state)
+
+    weights = []
+    for t in range(tiles):
+        live = jnp.where(lane < cells[t], 1.0, 0.0)
+        weights.append(volumes[:, t * LANES:(t + 1) * LANES] * live * scale_norm)
+    lowest, done = SLOTS, {stage: SLOTS for stage in range(1, 2 * STEPS + 1)}
+    for bottom, ids in ((6, ()), (4, (0, 1)), (0, (2, 3, 4, 5))):
+        arrive(ids)
+        for p in range(lowest - 1, bottom - 1, -1):
+            unpack(p)
+        if lowest == SLOTS:
+            swap_middle(state)
+        lowest = bottom
+        for stage in range(1, 2 * STEPS + 1):
+            start = min(bottom + stage, SLOTS)
+            for p in range(start, done[stage]):
+                advance(stage, p)
+            done[stage] = start
 
     direct_rows = []
     for g in range(fields):
         for t in range(tiles):
             e = 6 + t
             p, row = (e, 0) if e < SLOTS else (15 - e, 4)
-            live = jnp.where(lane < cells[t], 1.0, 0.0)
-            weight = volumes[:, t * LANES:(t + 1) * LANES] * live * scale_norm
             column = pl.ds(g * span + t * LANES, LANES)
-            direct_rows.append(weight * state[p, g, row:row + 2, :])
+            direct_rows.append(weights[t] * state[p, g, row:row + 2, :])
             adj_rows[0:2, column] = state[p, g, row + 2:row + 4, :]
     messages[mine] = jnp.concatenate(direct_rows, axis=1).astype(jnp.bfloat16)
 
@@ -283,14 +296,6 @@
     lax.fori_loop(1, n_blk, wait_sent, 0, unroll=few)
 
 
-UNROLL = True
-
-
-def finish(pair_in, bank_in, pair_out, bank_out):
-    pair_out[...] = pair_in[...]
-    bank_out[...] = bank_in[...]
-
-
 def local(n_blk, n_col, direct_init, adjoint_init, jacobian, areas, volumes, neighbours, block_cells, bank):
     fields, own, cell_count = direct_init.shape
     count = bank.shape[0]
@@ -302,8 +307,8 @@
     pair, projected = pl.pallas_call(
         functools.partial(kernel, n_blk, n_col, scale_norm),
         out_shape=(
-            jax.ShapeDtypeStruct((own, n_col * own), f32),
-            jax.ShapeDtypeStruct((n_col * own, count), f32),
+            pltpu.VMEM((own, n_col * own), f32),
+            pltpu.VMEM((n_col * own, count), f32),
         ),
         in_specs=[pl.BlockSpec(memory_space=pl.ANY)] * 8,
         out_specs=(vmem, vmem),
@@ -329,21 +334,11 @@
             pltpu.VMEM(neighbours.shape, jnp.int32),
             pltpu.VMEM((fields, count, cell_count), jnp.bfloat16),
             dma((8,)),
-            dma((4,)), dma((4,)), dma((n_col,)), dma((n_col,)), dma((n_blk,)), dma((n_blk,)),
+            dma((6,)), dma((6,)), dma((n_col,)), dma((n_col,)), dma((n_blk,)), dma((n_blk,)),
         ],
         compiler_params=pltpu.CompilerParams(collective_id=0, has_side_effects=True),
         name="hankel",
     )(jacobian, block_cells, direct_init, adjoint_init, areas, volumes.reshape(1, cell_count), neighbours, bank.transpose(1, 0, 2))
-    pair, projected = pl.pallas_call(
-        finish,
-        out_shape=(
-            jax.ShapeDtypeStruct((own, n_col * own), f32),
-            jax.ShapeDtypeStruct((n_col * own, count), f32),
-        ),
-        in_specs=[vmem, vmem],
-        out_specs=(vmem, vmem),
-        name="finish",
-    )(pair, projected)
     return pair.T, projected
 
 

time: 22.8 us -> 21.8 us (0.956)
  Pallas kernels: 22 us -> 19.9 us
  local copies, waits for them, and re-layouts: 0 us -> 1.16 us
    pallas_call x1 -> x0, Pallas kernels: 1.28 us -> none  [local(): pl.pallas_call(finish, out_shape=(jax.ShapeDtypeStruct((own, n_col * own)...]
    unnamed x0 -> x2, local copies, waits for them, and re-layouts: none -> 1.16 us
    pallas_call x1, Pallas kernels: 20.7 us -> 19.9 us  [local(): pl.pallas_call(functools.partial(kernel, n_blk, n_col, scale_norm), out_s...]
where the time goes in v2:
time: 21.8 us; the launch traced here: 21.7 us
  Pallas kernels  19.9 us (91%)
  local copies, waits for them, and re-layouts  1.16 us (5%)
  between operations  0.64 us (3%)
    pallas_call x1, Pallas kernels, local(): pl.pallas_call(functools.partial(kernel, n_blk, n_col, scale_norm), out_s...  19.9 us
    unnamed x2, local copies, waits for them, and re-layouts  1.16 us

profile of v2, /device:TPU:0, one launch (start us, length us, event | category | flops | bytes accessed | tf_op | source)
XLA Modules:
  0.0 21.7 jit_solution(4609320336437077876)
XLA Ops:
  0.6 19.9 %hankel.1 = (f32[2,8]{1,0:T(2,128)S(1)}, f32[8,32]{1,0:T(8,128)S(1)}) custom-call(f32[5,5]{1,0:T(8,128)} %jac_in.1, s32[4]{0:T(128)} %cells_in.1, f32[5,2,512]{2,1,0:T(2,128)} %direct_in.1, f32[5,2,512]{2,1,0:T(2,128)} %adjoint_in.1, f32[6,512]{1,0:T(8,128)} %areas_in.1, f32[1,512]{1,0:T(1,128)} %bitcast.5, s32[6,512]{1,0:T(8,128)} %neighbours_in.1, ...), custom_call_target="tpu_custom_call" | custom-call | tf_op jit(solution)/shard_map/hankel/pallas_call | solution.py:307
  20.5 0.6 %copy.12 = f32[8,2]{0,1:T(2,128)} copy(f32[8,2]{0,1:T(2,128)S(1)} %bitcast.3) | data formatting | bytes 128
  21.1 0.6 %copy.13 = f32[8,32]{1,0:T(8,128)} copy(f32[8,32]{1,0:T(8,128)S(1)} %get-tuple-element.7) | data formatting | bytes 2048

commit v3 on v2

--- a/solution.py
+++ b/solution.py
@@ -276,7 +276,11 @@
         return carry
 
     few = n_blk <= 16
-    lax.fori_loop(1, n_blk, start_sum, 0, unroll=few)
+    if few:
+        for step in sorted(range(1, n_blk), key=lambda i: -min(i, n_blk - i)):
+            start_sum(step, 0)
+    else:
+        lax.fori_loop(1, n_blk, start_sum, 0)
     lax.fori_loop(1, n_blk, wait_sum, 0, unroll=few)
     total = lax.fori_loop(
         0, n_blk, lambda i, total: total + parts[i], jnp.zeros(parts.shape[1:], jnp.float32), unroll=few

time: 21.8 us -> 21.8 us (level)
  no operation moved by 1% of the time
where the time goes in v3:
time: 21.8 us; the launch traced here: 21.7 us
  Pallas kernels  19.9 us (91%)
  local copies, waits for them, and re-layouts  1.16 us (5%)
  between operations  0.64 us (3%)
    pallas_call x1, Pallas kernels, local(): pl.pallas_call(functools.partial(kernel, n_blk, n_col, scale_norm), out_s...  19.9 us
    unnamed x2, local copies, waits for them, and re-layouts  1.16 us

profile of v3, /device:TPU:0, one launch (start us, length us, event | category | flops | bytes accessed | tf_op | source)
XLA Modules:
  0.0 21.7 jit_solution(8621060428064064622)
XLA Ops:
  0.6 19.9 %hankel.1 = (f32[2,8]{1,0:T(2,128)S(1)}, f32[8,32]{1,0:T(8,128)S(1)}) custom-call(f32[5,5]{1,0:T(8,128)} %jac_in.1, s32[4]{0:T(128)} %cells_in.1, f32[5,2,512]{2,1,0:T(2,128)} %direct_in.1, f32[5,2,512]{2,1,0:T(2,128)} %adjoint_in.1, f32[6,512]{1,0:T(8,128)} %areas_in.1, f32[1,512]{1,0:T(1,128)} %bitcast.5, s32[6,512]{1,0:T(8,128)} %neighbours_in.1, ...), custom_call_target="tpu_custom_call" | custom-call | tf_op jit(solution)/shard_map/hankel/pallas_call | solution.py:311
  20.5 0.6 %copy.12 = f32[8,2]{0,1:T(2,128)} copy(f32[8,2]{0,1:T(2,128)S(1)} %bitcast.3) | data formatting | bytes 128
  21.1 0.6 %copy.13 = f32[8,32]{1,0:T(8,128)} copy(f32[8,32]{1,0:T(8,128)S(1)} %get-tuple-element.7) | data formatting | bytes 2048
